TPU v7x, 32 devices: a whole 2x2x4 slice. The times are simulated.
32 devices in a mesh: row: 4 (over z), col: 4 (over y, x), feat: 2 (over core).
Axes of the slice: x: 2, y: 2, z: 4, core: 2. Of those that a mesh axis runs over, the one named last changes fastest.
Arguments:
- tile_values: bfloat16 [4, 4, 80, 128, 128], P('row', 'col')
- tile_rows: int32 [4, 4, 80], P('row', 'col'), may hold values from 0 to 15, as said below
- tile_cols: int32 [4, 4, 80], P('row', 'col'), may hold values from 0 to 15
- tile_mask: int32 [4, 4, 80], P('row', 'col'), may hold values from 0 to 1, as said below
- degree_caps: int32 [8192], P(('row', 'col')), may hold values from 1 to 32, as said below
- clip_groups: int32 [8192], P(('row', 'col')), may hold values from 0 to 7
- clip_bounds: float32 [8], replicated, may hold values from 51.2 to 256
- features: bfloat16 [8192, 256], P('col', 'feat')
- weight: bfloat16 [256, 256], replicated, may hold values from -0.375 to 0.375
- out_grad: bfloat16 [8192, 256], P(('row', 'col'), 'feat')
- dp_noise: float32 [256, 256], P(None, 'feat'), may hold values from -6 to 6
Outputs:
- out_feat: bfloat16 [8192, 256], P(('row', 'col'), 'feat')
- grad_weight: float32 [256, 256], P(None, 'feat')
- grad_input: bfloat16 [8192, 256], P('col', 'feat')
Inputs may be any that keep to these rules, and one draw needn't show every extreme that they name: `tile_rows`: each tile slot of one pair of row and col indices names a distinct pair of block row and block column. `tile_mask`: at most all 80 slots of one pair of row and col indices are live; in every draw some pair has all of them live. degree_caps[i] is the number of nonzero entries in row i of A, raised to 1 where it is 0 and capped at 32.
All inputs are finite; a program needn't handle non-finite values.
Results may differ from a plain program's by a relative error of at most 0.006.
Values may be sent and summed in bfloat16 or wider, within the bound.
A program may use at most 128 MiB of HBM per device.

v0:
```python
import math
import jax
import jax.numpy as jnp
from jax import lax
from jax.sharding import PartitionSpec as P


def slot_products(tile_vals, take_ids, source, flipped):
    contraction = "kji,kjf->kif" if flipped else "kij,kjf->kif"
    slot_total = tile_vals.shape[0]
    picked = jnp.take(source, take_ids, axis=0)
    products = jnp.einsum(contraction, tile_vals, picked, preferred_element_type=jnp.float32)
    return (products, jnp.arange(slot_total, dtype=jnp.int32))


def block_sums(products, put_ids, live_slots, block_count):
    wanted = jnp.arange(block_count, dtype=jnp.int32)
    selector = ((put_ids[:, None] == wanted[None, :]) & live_slots[:, None]).astype(jnp.float32)
    return jnp.einsum("kb,kif->bif", selector, products, precision=lax.Precision.HIGHEST)


def per_device(
    tile_values,
    tile_rows,
    tile_cols,
    tile_mask,
    degree_caps,
    clip_groups,
    clip_bounds,
    features,
    weight,
    out_grad,
    dp_noise,
):
    tile_vals = tile_values[0, 0]
    row_ids = tile_rows[0, 0]
    col_ids = tile_cols[0, 0]
    tile_live = tile_mask[0, 0]
    block_size = tile_vals.shape[1]
    half_width = features.shape[1]
    node_count = out_grad.shape[0]
    col_devices = lax.axis_size("col")
    row_devices = lax.axis_size("row")
    row_blocks = node_count * col_devices // block_size
    col_blocks = features.shape[0] // block_size
    grad_scale = 1.0 / math.sqrt(node_count * col_devices * row_devices)
    source = features.reshape(col_blocks, block_size, half_width)
    products, order = slot_products(tile_vals, col_ids, source, False)
    put_rows = jnp.take(row_ids, order)
    live_rows = jnp.take(tile_live, order) == 1
    partial_value = block_sums(products, put_rows, live_rows, row_blocks)
    partial_value = partial_value.reshape(row_blocks * block_size, half_width)
    summed = lax.psum_scatter(partial_value, "col", scatter_dimension=0, tiled=True)
    node_scale = lax.rsqrt(degree_caps.astype(jnp.float32))[:, None]
    agg_half = (summed * node_scale).astype(jnp.bfloat16)
    aggregate = lax.all_gather(agg_half, "feat", axis=1, tiled=True)
    feat_idx = lax.axis_index("feat")
    weight_cols = lax.dynamic_slice_in_dim(weight, feat_idx * half_width, half_width, 1)
    weight_rows = lax.dynamic_slice_in_dim(weight, feat_idx * half_width, half_width, 0)
    pre_act = jnp.dot(aggregate, weight_cols, preferred_element_type=jnp.float32)
    out_feat = jax.nn.silu(pre_act).astype(jnp.bfloat16)
    gate_sig = jax.nn.sigmoid(pre_act)
    grad_pre = (
        out_grad.astype(jnp.float32) * gate_sig * (1.0 + pre_act * (1.0 - gate_sig))
    ).astype(jnp.bfloat16)
    grad_full = lax.all_gather(grad_pre, "feat", axis=1, tiled=True)
    agg_sq = jnp.sum(jnp.square(aggregate.astype(jnp.float32)), axis=1)
    grad_sq = jnp.sum(jnp.square(grad_full.astype(jnp.float32)), axis=1)
    group_hits = (
        clip_groups[:, None] == jnp.arange(clip_bounds.shape[0], dtype=jnp.int32)[None, :]
    ).astype(jnp.float32)
    bounds = jnp.sum(group_hits * clip_bounds[None, :], axis=1)
    factor = jnp.minimum(1.0, bounds / (jnp.sqrt(agg_sq + 1e-06) * jnp.sqrt(grad_sq + 1e-06)))
    clipped = (factor[:, None] * grad_pre.astype(jnp.float32)).astype(jnp.bfloat16)
    local_grad = lax.dot_general(
        aggregate, clipped, (((0,), (0,)), ((), ())), preferred_element_type=jnp.float32
    )
    grad_weight = lax.psum(local_grad, ("row", "col")) * grad_scale + dp_noise
    back_prod = lax.dot_general(
        grad_full, weight_rows, (((1,), (1,)), ((), ())), preferred_element_type=jnp.float32
    )
    grad_agg = (back_prod * node_scale).astype(jnp.bfloat16)
    range_grads = lax.all_gather(grad_agg, "col", axis=0, tiled=True)
    grad_source = range_grads.reshape(row_blocks, block_size, half_width)
    back_products, back_order = slot_products(tile_vals, row_ids, grad_source, True)
    put_cols = jnp.take(col_ids, back_order)
    live_cols = jnp.take(tile_live, back_order) == 1
    input_part = block_sums(back_products, put_cols, live_cols, col_blocks)
    input_part = input_part.reshape(col_blocks * block_size, half_width)
    grad_input = lax.psum(input_part, "row").astype(jnp.bfloat16)
    return (out_feat, grad_weight, grad_input)


def solution(mesh):
    placed = (
        P("row", "col", None, None, None),
        P("row", "col", None),
        P("row", "col", None),
        P("row", "col", None),
        P(("row", "col")),
        P(("row", "col")),
        P(),
        P("col", "feat"),
        P(),
        P(("row", "col"), "feat"),
        P(None, "feat"),
    )
    return jax.shard_map(
        per_device,
        mesh=mesh,
        in_specs=placed,
        out_specs=(P(("row", "col"), "feat"), P(None, "feat"), P("col", "feat")),
        check_vma=False,
    )
```

profile of v0, /device:TPU:0, one launch (start us, length us, event | category | flops | bytes accessed | tf_op | source)
XLA Modules:
  0.0 184.9 jit_solution(5821199909000592426)
XLA Ops:
  7.2 0.0 copy-start
  7.2 0.0 copy-start.3
  7.2 0.0 reduce-scatter.2.cloned.1.call-start
  7.2 0.9 compare_and_fusion.1
  8.1 0.7 compare_select_fusion.1
  8.8 1.6 gather_fusion.1
  10.4 1.6 gather_fusion
  12.0 0.0 copy-done.3
  12.0 2.5 %gather_fusion.2 = bf16[80,128,128]{2,1,0:T(8,128)(2,1)} fusion(bf16[16,128,128]{2,1,0:T(8,128)(2,1)S(1)} %bitcast.41, s32[1024]{0:T(1024)S(1)} %pad_clamp_fusion.1), kind=kCustom, calls=%fused_computation.1.clone | custom fusion | bytes 5243200 | tf_op jit(solution)/shard_map/jit(_take)/gather | solution.py:11
  14.6 0.0 copy-done
  14.6 6.2 %fusion.8 = f32[80,128,128]{1,2,0:T(8,128)} fusion(bf16[1,1,80,128,128]{4,3,2,1,0:T(8,128)(2,1)S(1)} %copy-done, bf16[80,128,128]{2,1,0:T(8,128)(2,1)} %gather_fusion.2, pred[80]{0:T(512)(128)(4,1)S(1)} %compare_and_fusion.1), kind=kOutput, calls=%fused_computation.13 | convolution fusion | flops 336855040 | bytes 10485840 | tf_op jit(solution)/shard_map/kij,kjf->kif/dot_general | solution.py:12
  20.7 6.4 %copy.21 = f32[80,128,128]{2,0,1:T(8,128)} copy(f32[80,128,128]{1,2,0:T(8,128)} %fusion.8) | data formatting | bytes 10485760 | tf_op jit(solution)/shard_map/kij,kjf->kif/dot_general | solution.py:12
  27.1 4.3 %fusion.28 = f32[16,128,128]{2,0,1:T(8,128)S(1)} fusion(f32[80,128,128]{2,0,1:T(8,128)} %copy.21, s32[80]{0:T(128)S(1)} %broadcast_select_fusion.1, pred[80]{0:T(512)(128)(4,1)S(1)} %select_compare_fusion), kind=kOutput, calls=%fused_computation.38 | convolution fusion | flops 251660800 | bytes 6291856 | tf_op jit(solution)/shard_map/kb,kif->bif/dot_general | solution.py:19
  31.5 0.0 copy-start.1
  31.5 0.0 copy-start.2
  31.5 0.0 copy-start.6
  31.5 0.0 copy-start.8
  31.5 0.0 copy-start.7
  31.5 0.0 copy-start.5
  31.5 0.0 copy-start.9
  31.5 1.3 copy.22
  32.8 0.0 reduce-scatter.2.cloned.1.call-update
  32.9 0.0 all-reduce.3.cloned.1.call-start
  32.9 0.0 copy-done.1
  32.9 1.2 gather_fusion.3
  34.2 0.0 copy-done.2
  34.2 0.0 copy-done.6
  34.2 0.1 select_reduce_fusion
  34.3 29.1 %reduce-scatter.2.cloned.1.call-done = f32[512,128]{1,0:T(8,128)} async-done(((f32[2048,128]{1,0:T(8,128)}), f32[512,128]{1,0:T(8,128)}) %reduce-scatter.2.cloned.1.call-update) | async-done | bytes 262160 | tf_op jit(solution)/shard_map/reduce_scatter | solution.py:53
  63.4 1.1 multiply_convert_fusion.3
  64.5 2.0 %all_gather.9 = bf16[512,256]{1,0:T(8,128)(2,1)S(1)} all-gather(bf16[512,128]{1,0:T(8,128)(2,1)S(1)} %multiply_convert_fusion.3), channel_id=1, replica_groups=mesh['row'=4,'col'=4,'feat'=2] {'feat'}, dimensions={1}, use_global_device_ids=true | all-gather | bytes 393216 | tf_op jit(solution)/shard_map/all_gather | solution.py:56
  66.5 0.1 multiply_reduce_fusion.1
  66.7 1.0 multiply_convert_fusion.1
  67.7 2.0 %all_gather.10 = bf16[512,256]{1,0:T(8,128)(2,1)S(1)} all-gather(bf16[512,128]{1,0:T(8,128)(2,1)S(1)} %get-tuple-element.5), channel_id=1, replica_groups=mesh['row'=4,'col'=4,'feat'=2] {'feat'}, dimensions={1}, use_global_device_ids=true | all-gather | bytes 393216 | tf_op jit(solution)/shard_map/all_gather | solution.py:66
  69.6 0.1 multiply_reduce_fusion
  69.8 0.2 fusion.20
  70.0 1.0 fusion.21
  71.1 0.0 all-reduce.3.cloned.1.call-update
  71.1 10.2 %all_gather.11 = bf16[2048,128]{1,0:T(8,128)(2,1)S(1)} all-gather(bf16[512,128]{1,0:T(8,128)(2,1)S(1)} %fusion.20), channel_id=1, replica_groups=mesh['row'=4,'col'=4,'feat'=2] {'col'}, dimensions={0}, use_global_device_ids=true | all-gather | bytes 655360 | tf_op jit(solution)/shard_map/all_gather | solution.py:83
  81.3 2.5 %gather_fusion.4 = bf16[80,128,128]{2,1,0:T(8,128)(2,1)} fusion(bf16[16,128,128]{2,1,0:T(8,128)(2,1)S(1)} %bitcast.40, s32[1024]{0:T(1024)S(1)} %pad_clamp_fusion), kind=kCustom, calls=%fused_computation.4.clone | custom fusion | bytes 5243200 | tf_op jit(solution)/shard_map/jit(_take)/gather | solution.py:11
  83.8 5.2 %fusion.13 = f32[80,128,128]{1,2,0:T(8,128)} fusion(bf16[1,1,80,128,128]{4,3,2,1,0:T(8,128)(2,1)S(1)} %copy-done, bf16[80,128,128]{2,1,0:T(8,128)(2,1)} %gather_fusion.4, pred[80]{0:T(512)(128)(4,1)S(1)} %compare_and_fusion), kind=kOutput, calls=%fused_computation.14 | convolution fusion | flops 336855040 | bytes 10485840 | tf_op jit(solution)/shard_map/kji,kjf->kif/dot_general | solution.py:12
  89.0 6.4 %copy.24 = f32[80,128,128]{2,0,1:T(8,128)} copy(f32[80,128,128]{1,2,0:T(8,128)} %fusion.13) | data formatting | bytes 10485760 | tf_op jit(solution)/shard_map/kji,kjf->kif/dot_general | solution.py:12
  95.4 4.3 %fusion.32 = f32[16,128,128]{2,0,1:T(8,128)S(1)} fusion(f32[80,128,128]{2,0,1:T(8,128)} %copy.24, s32[80]{0:T(128)S(1)} %broadcast_select_fusion, pred[80]{0:T(512)(128)(4,1)S(1)} %select_compare_fusion), kind=kOutput, calls=%fused_computation.41 | convolution fusion | flops 251660800 | bytes 6291856 | tf_op jit(solution)/shard_map/kb,kif->bif/dot_general | solution.py:19
  99.8 0.0 copy-start.4
  99.8 1.3 copy.25
  101.1 44.6 %all-reduce.4 = bf16[2048,128]{1,0:T(8,128)(2,1)} all-reduce(f32[2048,128]{1,0:T(8,128)} %bitcast.43), channel_id=1, replica_groups=mesh['row'=4,'col'=4,'feat'=2] {'row'}, use_global_device_ids=true, to_apply=%region_5.8 | all-reduce | flops 262144 | bytes 1572864 | tf_op jit(solution)/shard_map/psum | solution.py:90
  145.7 30.7 %all-reduce.3.cloned.1.call-done = f32[256,128]{1,0:T(8,128)} async-done(((f32[256,128]{1,0:T(8,128)}), f32[256,128]{1,0:T(8,128)}) %all-reduce.3.cloned.1.call-update) | async-done | bytes 131088 | tf_op jit(solution)/shard_map/psum | solution.py:78
  176.5 1.6 multiply_add_fusion
  (16 shorter events, 0.1 us)
Async XLA Ops:
  7.2 7.4 %copy-start = (bf16[1,1,80,128,128]{4,3,2,1,0:T(8,128)(2,1)S(1)}, bf16[1,1,80,128,128]{4,3,2,1,0:T(8,128)(2,1)}, u32[]{:S(2)}) copy-start(bf16[1,1,80,128,128]{4,3,2,1,0:T(8,128)(2,1)} %param.15) | copy-start | bytes 7864324
  7.2 4.8 %copy-start.3 = (bf16[2048,128]{1,0:T(8,128)(2,1)S(1)}, bf16[2048,128]{1,0:T(8,128)(2,1)}, u32[]{:S(2)}) copy-start(bf16[2048,128]{1,0:T(8,128)(2,1)} %param.22) | copy-start | bytes 1572868
  7.2 56.3 %reduce-scatter.2.cloned.1.call-start = ((), (), s32[]{:S(2)}) async-start(), calls=%async_computation.1 | async-start | bytes 1310720 | tf_op jit(solution)/shard_map/reduce_scatter | solution.py:53
  31.5 1.5 copy-start.1
  31.5 2.7 %copy-start.2 = (s32[1,1,80]{2,1,0:T(1,128)S(1)}, s32[1,1,80]{2,1,0:T(1,128)}, u32[]{:S(2)}) copy-start(s32[1,1,80]{2,1,0:T(1,128)} %param.16) | copy-start | bytes 964
  31.5 2.7 %copy-start.6 = (s32[512]{0:T(512)S(1)}, s32[512]{0:T(512)}, u32[]{:S(2)}) copy-start(s32[512]{0:T(512)} %param.20) | copy-start | bytes 6148
  31.5 2.7 %copy-start.8 = (f32[8]{0:T(128)S(1)}, f32[8]{0:T(128)}, u32[]{:S(2)}) copy-start(f32[8]{0:T(128)} %param.21) | copy-start | bytes 100
  31.5 2.8 %copy-start.7 = (s32[512]{0:T(512)S(1)}, s32[512]{0:T(512)}, u32[]{:S(2)}) copy-start(s32[512]{0:T(512)} %param.19) | copy-start | bytes 6148
  31.5 35.2 %copy-start.5 = (bf16[256,256]{1,0:T(8,128)(2,1)S(1)}, bf16[256,256]{1,0:T(8,128)(2,1)}, u32[]{:S(2)}) copy-start(bf16[256,256]{1,0:T(8,128)(2,1)} %param.23) | copy-start | bytes 393220
  31.5 35.2 %copy-start.9 = (bf16[512,128]{1,0:T(8,128)(2,1)S(1)}, bf16[512,128]{1,0:T(8,128)(2,1)}, u32[]{:S(2)}) copy-start(bf16[512,128]{1,0:T(8,128)(2,1)} %param.24) | copy-start | bytes 393220
  32.9 143.6 %all-reduce.3.cloned.1.call-start = ((), (), s32[]{:S(2)}) async-start(), calls=%async_computation.2 | async-start | bytes 262144 | tf_op jit(solution)/shard_map/psum | solution.py:78
  99.8 76.7 %copy-start.4 = (f32[256,128]{1,0:T(8,128)S(1)}, f32[256,128]{1,0:T(8,128)}, u32[]{:S(2)}) copy-start(f32[256,128]{1,0:T(8,128)} %param.25) | copy-start | bytes 393220
Sparse Core Ops, SparseCore 0:
  33.0 30.4 reduce-scatter.1
  71.2 105.2 all-reduce.2
where the time goes:
time: 185 us
  waiting for transfers between devices  59.9 us (32%)
  blocking collectives  58.8 us (32%)
  local copies, waits for them, and re-layouts  24.9 us (13%)
  matrix products  22.3 us (12%)
  between operations  14.3 us (8%)
  other arithmetic  4.65 us (3%)
    psum x1, blocking collectives, per_device(): grad_input = lax.psum(input_part, 'row').astype(jnp.bfloat16)  44.6 us
    psum x1, waiting for transfers between devices, per_device(): grad_weight = lax.psum(local_grad, ('row', 'col')) * grad_scale + dp_noise  30.7 us
    reduce_scatter x1, waiting for transfers between devices, per_device(): lax.psum_scatter(partial_value, 'col', scatter_dimension=0, tiled=True)  29.1 us
    dot_general x2, local copies, waits for them, and re-layouts, slot_products(): jnp.einsum(contraction, tile_vals, picked, preferred_element_type=jnp.flo...  12.8 us
    dot_general x2, matrix products, slot_products(): jnp.einsum(contraction, tile_vals, picked, preferred_element_type=jnp.flo...  11.4 us
    all_gather x1, blocking collectives, per_device(): range_grads = lax.all_gather(grad_agg, 'col', axis=0, tiled=True)  10.2 us
    dot_general x2, matrix products, block_sums(): jnp.einsum('kb,kif->bif', selector, products, precision=lax.Precision.HIG...  8.69 us
    gather x2, local copies, waits for them, and re-layouts, slot_products(): picked = jnp.take(source, take_ids, axis=0)  5.08 us
  transfers between devices with their start and end apart: 2, of which 2 were waited for; matrix products, arithmetic and copies ran while one was open for 11% of the time, Pallas kernels for 0%

commit v1 on v0

--- a/solution.py
+++ b/solution.py
@@ -80,7 +80,24 @@
         grad_full, weight_rows, (((1,), (1,)), ((), ())), preferred_element_type=jnp.float32
     )
     grad_agg = (back_prod * node_scale).astype(jnp.bfloat16)
-    range_grads = lax.all_gather(grad_agg, "col", axis=0, tiled=True)
+    size, index, rows = (lax.axis_size("col"), lax.axis_index("col"), grad_agg.shape[0])
+    right = [(i, (i + 1) % size) for i in range(size)]
+    left = [(i, (i - 1) % size) for i in range(size)]
+    whole = jnp.zeros((*grad_agg.shape[:0], size * rows, *grad_agg.shape[0 + 1 :]), grad_agg.dtype)
+    whole = lax.dynamic_update_slice_in_dim(whole, grad_agg, index * rows, axis=0)
+    from_left = from_right = grad_agg
+    halfway = size // 2
+    for turn in range(1, halfway + 1):
+        from_left = lax.ppermute(from_left, "col", right)
+        whole = lax.dynamic_update_slice_in_dim(
+            whole, from_left, (index - turn) % size * rows, axis=0
+        )
+        if turn < size - halfway:
+            from_right = lax.ppermute(from_right, "col", left)
+            whole = lax.dynamic_update_slice_in_dim(
+                whole, from_right, (index + turn) % size * rows, axis=0
+            )
+    range_grads = whole
     grad_source = range_grads.reshape(row_blocks, block_size, half_width)
     back_products, back_order = slot_products(tile_vals, row_ids, grad_source, True)
     put_cols = jnp.take(col_ids, back_order)

time: 185 us -> 253 us (1.37)
  waiting for transfers between devices: 59.9 us -> 133 us
  blocking collectives: 58.8 us -> 46.6 us
  starting transfers between devices: 0.08 us -> 4.44 us
    psum x1, waiting for transfers between devices: 30.7 us -> 99.5 us  [per_device(): grad_weight = lax.psum(local_grad, ('row', 'col')) * grad_scale + dp_noise]
    all_gather x1 -> x0, blocking collectives: 10.2 us -> none  [per_device(): range_grads = lax.all_gather(grad_agg, 'col', axis=0, tiled=True)]
    ppermute x0 -> x3, waiting for transfers between devices: none -> 4.37 us  [the longest x2 4.37 us: per_device(): from_left = lax.ppermute(from_left, 'col', right)]
    ppermute x0 -> x3, starting transfers between devices: none -> 4.36 us  [the longest x2 2.84 us: per_device(): from_left = lax.ppermute(from_left, 'col', right)]
  transfers between devices with their start and end apart: 2 -> 5, of which waited for: 2 -> 3; matrix products, arithmetic and copies ran while one was open for 11% -> 2% of each run, Pallas kernels for 0% -> 0%
where the time goes in v1:
time: 253 us; the launch traced here: 252 us
  waiting for transfers between devices  133 us (53%)
  blocking collectives  46.6 us (18%)
  local copies, waits for them, and re-layouts  25.3 us (10%)
  matrix products  23.7 us (9%)
  between operations  14.3 us (6%)
  other arithmetic  5.1 us (2%)
  starting transfers between devices  4.44 us (2%)
    psum x1, waiting for transfers between devices, per_device(): grad_weight = lax.psum(local_grad, ('row', 'col')) * grad_scale + dp_noise  99.5 us
    psum x1, blocking collectives, per_device(): grad_input = lax.psum(input_part, 'row').astype(jnp.bfloat16)  42.6 us
    reduce_scatter x1, waiting for transfers between devices, per_device(): lax.psum_scatter(partial_value, 'col', scatter_dimension=0, tiled=True)  28.6 us
    dot_general x2, local copies, waits for them, and re-layouts, slot_products(): jnp.einsum(contraction, tile_vals, picked, preferred_element_type=jnp.flo...  12.8 us
    dot_general x2, matrix products, slot_products(): jnp.einsum(contraction, tile_vals, picked, preferred_element_type=jnp.flo...  11.3 us
    dot_general x2, matrix products, block_sums(): jnp.einsum('kb,kif->bif', selector, products, precision=lax.Precision.HIG...  8.69 us
    gather x2, local copies, waits for them, and re-layouts, slot_products(): picked = jnp.take(source, take_ids, axis=0)  6.1 us
  transfers between devices with their start and end apart: 5, of which 3 were waited for; matrix products, arithmetic and copies ran while one was open for 2% of the time, Pallas kernels for 0%

profile of v1, /device:TPU:0, one launch (start us, length us, event | category | flops | bytes accessed | tf_op | source)
XLA Modules:
  0.0 252.1 jit_solution(12405316663045354448)
XLA Ops:
  7.2 0.0 copy-start
  7.2 0.0 reduce-scatter.2.cloned.1.call-start
  7.2 0.8 compare_select_fusion.1
  8.0 0.7 compare_and_fusion
  8.7 3.6 %gather_fusion.2 = bf16[80,128,128]{2,1,0:T(8,128)(2,1)} fusion(bf16[16,128,128]{2,1,0:T(8,128)(2,1)} %bitcast.41, s32[1024]{0:T(1024)S(1)} %pad_clamp_fusion.1), kind=kCustom, calls=%fused_computation.1.clone | custom fusion | bytes 5243200 | tf_op jit(solution)/shard_map/jit(_take)/gather | solution.py:11
  12.3 6.1 %fusion.8 = f32[80,128,128]{1,2,0:T(8,128)} fusion(bf16[1,1,80,128,128]{4,3,2,1,0:T(8,128)(2,1)S(1)} %copy-done, bf16[80,128,128]{2,1,0:T(8,128)(2,1)} %gather_fusion.2, pred[80]{0:T(512)(128)(4,1)S(1)} %get-tuple-element.10), kind=kOutput, calls=%fused_computation.13 | convolution fusion | flops 336855040 | bytes 10485840 | tf_op jit(solution)/shard_map/kij,kjf->kif/dot_general | solution.py:12
  18.4 6.4 %copy.21 = f32[80,128,128]{2,0,1:T(8,128)} copy(f32[80,128,128]{1,2,0:T(8,128)} %fusion.8) | data formatting | bytes 10485760 | tf_op jit(solution)/shard_map/kij,kjf->kif/dot_general | solution.py:12
  24.8 0.0 copy-done.2
  24.9 1.2 gather_fusion
  26.1 1.2 gather_fusion.1
  27.4 4.3 %fusion.28 = f32[16,128,128]{2,0,1:T(8,128)S(1)} fusion(f32[80,128,128]{2,0,1:T(8,128)} %copy.21, s32[80]{0:T(128)S(1)} %broadcast_select_fusion.1, pred[80]{0:T(512)(128)(4,1)S(1)} %select_compare_fusion), kind=kOutput, calls=%fused_computation.38 | convolution fusion | flops 251660800 | bytes 6291856 | tf_op jit(solution)/shard_map/kb,kif->bif/dot_general | solution.py:19
  31.7 0.0 copy-start.1
  31.7 0.0 copy-start.6
  31.7 0.0 copy-start.8
  31.7 0.0 copy-start.7
  31.8 0.0 copy-start.5
  31.8 0.0 copy-start.10
  31.8 1.3 copy.22
  33.1 0.0 reduce-scatter.2.cloned.1.call-update
  33.1 0.0 all-reduce.3.cloned.1.call-start
  33.2 1.2 gather_fusion.3
  34.5 0.1 select_reduce_fusion
  34.6 0.5 broadcast_select_fusion
  35.1 28.6 %reduce-scatter.2.cloned.1.call-done = f32[512,128]{1,0:T(8,128)} async-done(((f32[2048,128]{1,0:T(8,128)}), f32[512,128]{1,0:T(8,128)}) %reduce-scatter.2.cloned.1.call-update) | async-done | bytes 262160 | tf_op jit(solution)/shard_map/reduce_scatter | solution.py:53
  63.8 1.1 multiply_convert_fusion.3
  64.8 2.0 all_gather.6
  66.8 0.1 multiply_reduce_fusion.1
  67.0 1.0 multiply_convert_fusion.1
  68.0 2.0 all_gather.7
  69.9 0.1 multiply_reduce_fusion
  70.1 1.0 fusion.21
  71.1 0.0 all-reduce.3.cloned.1.call-update
  71.2 0.1 broadcast_in_dim.17
  71.2 1.8 constant_dynamic-update-slice_fusion.3
  73.0 1.4 collective-permute-start
  74.4 1.5 collective-permute-start.1
  75.9 99.5 %all-reduce.3.cloned.1.call-done = f32[256,128]{1,0:T(8,128)} async-done(((f32[256,128]{1,0:T(8,128)}), f32[256,128]{1,0:T(8,128)}) %all-reduce.3.cloned.1.call-update) | async-done | bytes 131088 | tf_op jit(solution)/shard_map/psum | solution.py:78
  175.4 1.6 multiply_add_fusion
  177.0 0.0 collective-permute-done
  177.0 1.4 collective-permute-start.2
  178.5 0.0 collective-permute-done.1
  178.5 4.4 %collective-permute-done.2 = bf16[512,128]{1,0:T(8,128)(2,1)S(1)} collective-permute-done((bf16[512,128]{1,0:T(8,128)(2,1)S(1)}, bf16[512,128]{1,0:T(8,128)(2,1)S(1)}, u32[]{:S(2)}, u32[]{:S(2)}) %collective-permute-start.2) | collective-permute-done | bytes 131104 | tf_op jit(solution)/shard_map/ppermute | solution.py:91
  182.9 2.5 %gather_fusion.4 = bf16[80,128,128]{2,1,0:T(8,128)(2,1)} fusion(bf16[16,128,128]{2,1,0:T(8,128)(2,1)S(1)} %bitcast.40, s32[1024]{0:T(1024)S(1)} %pad_clamp_fusion), kind=kCustom, calls=%fused_computation.4.clone | custom fusion | bytes 5243200 | tf_op jit(solution)/shard_map/jit(_take)/gather | solution.py:11
  185.4 5.2 %fusion.13 = f32[80,128,128]{1,2,0:T(8,128)} fusion(bf16[1,1,80,128,128]{4,3,2,1,0:T(8,128)(2,1)S(1)} %copy-done, bf16[80,128,128]{2,1,0:T(8,128)(2,1)} %gather_fusion.4, pred[80]{0:T(512)(128)(4,1)S(1)} %get-tuple-element.9), kind=kOutput, calls=%fused_computation.14 | convolution fusion | flops 336855040 | bytes 10485840 | tf_op jit(solution)/shard_map/kji,kjf->kif/dot_general | solution.py:12
  190.6 6.4 %copy.24 = f32[80,128,128]{2,0,1:T(8,128)} copy(f32[80,128,128]{1,2,0:T(8,128)} %fusion.13) | data formatting | bytes 10485760 | tf_op jit(solution)/shard_map/kji,kjf->kif/dot_general | solution.py:12
  197.0 4.3 %fusion.32 = f32[16,128,128]{2,0,1:T(8,128)S(1)} fusion(f32[80,128,128]{2,0,1:T(8,128)} %copy.24, s32[80]{0:T(128)S(1)} %copy-done.9, pred[80]{0:T(512)(128)(4,1)S(1)} %select_compare_fusion), kind=kOutput, calls=%fused_computation.41 | convolution fusion | flops 251660800 | bytes 6291856 | tf_op jit(solution)/shard_map/kb,kif->bif/dot_general | solution.py:19
  201.3 1.3 copy.25
  202.6 42.6 %all-reduce.4 = bf16[2048,128]{1,0:T(8,128)(2,1)} all-reduce(f32[2048,128]{1,0:T(8,128)} %bitcast.43), channel_id=1, replica_groups=mesh['row'=4,'col'=4,'feat'=2] {'row'}, use_global_device_ids=true, to_apply=%region_5.8 | all-reduce | flops 262144 | bytes 1572864 | tf_op jit(solution)/shard_map/psum | solution.py:107
  (26 shorter events, 0.1 us)
Async XLA Ops:
  7.2 5.1 %copy-start = (bf16[1,1,80,128,128]{4,3,2,1,0:T(8,128)(2,1)S(1)}, bf16[1,1,80,128,128]{4,3,2,1,0:T(8,128)(2,1)}, u32[]{:S(2)}) copy-start(bf16[1,1,80,128,128]{4,3,2,1,0:T(8,128)(2,1)} %param.15) | copy-start | bytes 7864324
  7.2 56.6 %reduce-scatter.2.cloned.1.call-start = ((), (), s32[]{:S(2)}) async-start(), calls=%async_computation.1 | async-start | bytes 1310720 | tf_op jit(solution)/shard_map/reduce_scatter | solution.py:53
  18.4 6.4 %copy-start.2 = (s32[1,1,80]{2,1,0:T(1,128)S(1)}, s32[1,1,80]{2,1,0:T(1,128)}, u32[]{:S(2)}) copy-start(s32[1,1,80]{2,1,0:T(1,128)} %param.16) | copy-start | bytes 964
  18.4 7.7 %copy-start.3 = (s32[1,1,80]{2,1,0:T(1,128)S(1)}, s32[1,1,80]{2,1,0:T(1,128)}, u32[]{:S(2)}) copy-start(s32[1,1,80]{2,1,0:T(1,128)} %param.18) | copy-start | bytes 964
  31.7 1.5 copy-start.1
  31.7 2.8 %copy-start.6 = (s32[512]{0:T(512)S(1)}, s32[512]{0:T(512)}, u32[]{:S(2)}) copy-start(s32[512]{0:T(512)} %param.20) | copy-start | bytes 6148
  31.7 2.8 %copy-start.8 = (f32[8]{0:T(128)S(1)}, f32[8]{0:T(128)}, u32[]{:S(2)}) copy-start(f32[8]{0:T(128)} %param.21) | copy-start | bytes 100
  31.7 3.4 %copy-start.7 = (s32[512]{0:T(512)S(1)}, s32[512]{0:T(512)}, u32[]{:S(2)}) copy-start(s32[512]{0:T(512)} %param.19) | copy-start | bytes 6148
  31.8 35.2 %copy-start.5 = (bf16[256,256]{1,0:T(8,128)(2,1)S(1)}, bf16[256,256]{1,0:T(8,128)(2,1)}, u32[]{:S(2)}) copy-start(bf16[256,256]{1,0:T(8,128)(2,1)} %param.23) | copy-start | bytes 393220
  31.8 35.2 %copy-start.10 = (bf16[512,128]{1,0:T(8,128)(2,1)S(1)}, bf16[512,128]{1,0:T(8,128)(2,1)}, u32[]{:S(2)}) copy-start(bf16[512,128]{1,0:T(8,128)(2,1)} %param.24) | copy-start | bytes 393220
  33.1 142.3 %all-reduce.3.cloned.1.call-start = ((), (), s32[]{:S(2)}) async-start(), calls=%async_computation.2 | async-start | bytes 262144 | tf_op jit(solution)/shard_map/psum | solution.py:78
  35.1 140.3 %copy-start.4 = (f32[256,128]{1,0:T(8,128)S(1)}, f32[256,128]{1,0:T(8,128)}, u32[]{:S(2)}) copy-start(f32[256,128]{1,0:T(8,128)} %param.25) | copy-start | bytes 393220
  73.0 104.0 %collective-permute-start = (bf16[512,128]{1,0:T(8,128)(2,1)}, bf16[512,128]{1,0:T(8,128)(2,1)S(1)}, u32[]{:S(2)}, u32[]{:S(2)}) collective-permute-start(bf16[512,128]{1,0:T(8,128)(2,1)} %get-tuple-element.8), channel_id=1, source_target_pairs={{0,2},{2,4},{4,6},{6,0},{1,3},{3,5},{5,7},{7,1},{8,10},{10,12},{12... | collective-permute-start | bytes 393224 | tf_op jit(solution)/shard_map/ppermute | solution.py:91
  74.4 104.1 %collective-permute-start.1 = (bf16[512,128]{1,0:T(8,128)(2,1)}, bf16[512,128]{1,0:T(8,128)(2,1)S(1)}, u32[]{:S(2)}, u32[]{:S(2)}) collective-permute-start(bf16[512,128]{1,0:T(8,128)(2,1)} %get-tuple-element.8), channel_id=1, source_target_pairs={{0,6},{2,0},{4,2},{6,4},{1,7},{3,1},{5,3},{7,5},{8,14},{10,8},{12,... | collective-permute-start | bytes 393224 | tf_op jit(solution)/shard_map/ppermute | solution.py:96
  177.0 5.9 %collective-permute-start.2 = (bf16[512,128]{1,0:T(8,128)(2,1)S(1)}, bf16[512,128]{1,0:T(8,128)(2,1)S(1)}, u32[]{:S(2)}, u32[]{:S(2)}) collective-permute-start(bf16[512,128]{1,0:T(8,128)(2,1)S(1)} %collective-permute-done), channel_id=1, source_target_pairs={{0,2},{2,4},{4,6},{6,0},{1,3},{3,5},{5,7},{7,1},{8,10},{10,12},{12... | collective-permute-start | bytes 393224 | tf_op jit(solution)/shard_map/ppermute | solution.py:91
  190.6 6.4 %copy-start.9 = (s32[80]{0:T(128)S(1)}, s32[80]{0:T(128)}, u32[]{:S(2)}) copy-start(s32[80]{0:T(128)} %broadcast_select_fusion) | copy-start | bytes 964
Sparse Core Ops, SparseCore 0:
  33.2 30.4 reduce-scatter.1
  71.3 104.1 all-reduce.2
